TPU v7x, 32 devices: a whole 2x2x4 slice. The times are simulated.
32 devices in a mesh: img: 8 (over z, y), seq: 4 (over x, core).
Axes of the slice: x: 2, y: 2, z: 4, core: 2. Of those that a mesh axis runs over, the one named last changes fastest.
Arguments:
- tokens: float32 [8, 4096, 384], P('img', 'seq'), may hold values from -6 to 6
- valid_mask: int32 [8, 4096], P('img', 'seq'), may hold values from 0 to 1, as said below
- timesteps: int32 [8], P('img'), may hold values from 0 to 999
- class_ids: int32 [8], P('img'), may hold values from 0 to 999
- time_first: float32 [256, 384], replicated, may hold values from -0.375 to 0.375
- time_second: float32 [384, 384], replicated, may hold values from -0.3125 to 0.3125
- class_table: float32 [1000, 384], replicated, may hold values from -6 to 6
- ada_weight: float32 [384, 2304], replicated, may hold values from -0.3125 to 0.3125
- ada_bias: float32 [2304], replicated, may hold values from -3 to 3
- conv_taps: float32 [9, 384], replicated, may hold values from -2 to 2
- query_proj: float32 [384, 384], replicated, may hold values from -0.3125 to 0.3125
- key_proj: float32 [384, 384], replicated, may hold values from -0.3125 to 0.3125
- value_proj: float32 [384, 384], replicated, may hold values from -0.3125 to 0.3125
- decay_down: float32 [384, 16], replicated, may hold values from -0.3125 to 0.3125
- decay_up: float32 [16, 384], replicated, may hold values from -1.5 to 1.5
- decay_bias: float32 [384], replicated, may hold values from 0.5 to 6
- gate_proj: float32 [384, 384], replicated, may hold values from -0.3125 to 0.3125
- out_proj: float32 [384, 384], replicated, may hold values from -0.625 to 0.625
- mlp_up: float32 [384, 1536], replicated, may hold values from -0.3125 to 0.3125
- mlp_down: float32 [1536, 384], replicated, may hold values from -0.3125 to 0.3125
- cotangent: float32 [8, 4096, 384], P('img', 'seq'), may hold values from -6 to 6
Outputs:
- block_out: float32 [8, 4096, 384], P('img', 'seq')
- tokens_grad: float32 [8, 4096, 384], P('img', 'seq')
- time_first_grad: float32 [256, 384], replicated
- time_second_grad: float32 [384, 384], replicated
- class_table_grad: float32 [1000, 384], replicated
- ada_weight_grad: float32 [384, 2304], replicated
- ada_bias_grad: float32 [2304], replicated
- conv_taps_grad: float32 [9, 384], replicated
- query_proj_grad: float32 [384, 384], replicated
- key_proj_grad: float32 [384, 384], replicated
- value_proj_grad: float32 [384, 384], replicated
- decay_down_grad: float32 [384, 16], replicated
- decay_up_grad: float32 [16, 384], replicated
- decay_bias_grad: float32 [384], replicated
- gate_proj_grad: float32 [384, 384], replicated
- out_proj_grad: float32 [384, 384], replicated
- mlp_up_grad: float32 [384, 1536], replicated
- mlp_down_grad: float32 [1536, 384], replicated
Inputs may be any that keep to these rules, and one draw needn't show every extreme that they name: `valid_mask`: in each image the real patches are the first L of its 4096 patches, with 1024 <= L < 4096.
All inputs are finite; a program needn't handle non-finite values.
Results may differ from a plain program's by a relative error of at most 0.0003.
Values sent between devices are 32-bit elements; how exact they have to be, the bound alone decides.
No kernel may reach another device: no remote copies, remote signals or barrier semaphores. Data moves between devices by JAX's collectives and lax.ppermute only.
A program may use at most 320 MiB of HBM per device.

v0:
```python
import math
import jax
import jax.numpy as jnp
from jax import lax
from jax.sharding import PartitionSpec as P

HEADS = 6
HEAD_DIM = 64
CLASSES = 1000
FREQ = 256
GRID = 64
STRETCH = 64
HIGH = lax.Precision.HIGHEST


def extended(shard, sides, width):
    for axis, dim in sides:
        size, length = (lax.axis_size(axis), shard.shape[dim])
        up = [(i, (i + 1) % size) for i in range(size - 1)]
        down = [(j, i) for i, j in up]
        last = lax.slice_in_dim(shard, length - width, length, axis=dim)
        leading = lax.slice_in_dim(shard, 0, width, axis=dim)
        before = lax.ppermute(last, axis, up)
        after = lax.ppermute(leading, axis, down)
        shard = jnp.concatenate([before, shard, after], axis=dim)
    return shard


def carried_in(value, axis, join, neutral, backward):
    count, mine = (lax.axis_size(axis), lax.axis_index(axis))
    pieces = jax.tree.map(lambda part: lax.all_gather(part, axis), value)
    if backward:
        pieces = jax.tree.map(lambda part: part[::-1], pieces)
        mine = count - 1 - mine
    total = jax.tree.map(
        lambda part, zero: jnp.full_like(part, 0) + jnp.asarray(zero, part.dtype), value, neutral
    )

    def lap(position, total):
        longer = join(total, jax.tree.map(lambda part: part[position], pieces))
        return jax.tree.map(lambda new, old: jnp.where(position < mine, new, old), longer, total)

    return lax.fori_loop(0, count - 1, lap, total)


def product(left, right):
    return jnp.dot(left, right, precision=HIGH, preferred_element_type=jnp.float32)


def time_features(timesteps):
    half = FREQ // 2
    freqs = jnp.exp(-math.log(10000.0) * jnp.arange(half, dtype=jnp.float32) / half)
    angles = timesteps.astype(jnp.float32)[:, None] * freqs[None, :]
    return jnp.concatenate([jnp.cos(angles), jnp.sin(angles)], axis=1)


def condition(timesteps, class_ids, time_first, time_second, class_table, ada_weight, ada_bias):
    embed = product(jax.nn.silu(product(time_features(timesteps), time_first)), time_second)
    onehot = (class_ids[:, None] == jnp.arange(CLASSES, dtype=jnp.int32)[None, :]).astype(
        jnp.float32
    )
    embed = embed + product(onehot, class_table)
    return product(jax.nn.silu(embed), ada_weight) + ada_bias


def layer_norm(values):
    center = values - jnp.mean(values, axis=-1, keepdims=True)
    return center * lax.rsqrt(jnp.mean(center * center, axis=-1, keepdims=True) + 1e-06)


def pair_mix(query, keys, values, cumul):
    diff = cumul[..., :, None, :, :] - cumul[..., None, :, :, :]
    size = cumul.shape[-3]
    causal = (jnp.arange(size)[:, None] >= jnp.arange(size)[None, :])[:, :, None, None]
    weight = jnp.where(causal, jnp.exp(jnp.where(causal, diff, 0.0)), 0.0)
    scores = jnp.sum(query[..., :, None, :, :] * keys[..., None, :, :, :] * weight, axis=-1)
    return jnp.einsum("...tsh,...she->...the", scores, values, precision=HIGH)


def chain_join(earlier, later):
    return (later[0] * earlier[0], later[0][..., None] * earlier[1] + later[1])


def front(tokens, modul):
    pieces = jnp.split(modul, 6, axis=1)
    return layer_norm(tokens) * (1.0 + pieces[1][:, None]) + pieces[0][:, None]


def mixer_front(
    padded, keep, conv_taps, query_proj, key_proj, value_proj, decay_down, decay_up, decay_bias
):
    count, span, width = padded.shape
    length = span - 2 * GRID
    lines = length // GRID
    grid = jnp.pad(padded.reshape(count, lines + 2, GRID, width), ((0, 0), (0, 0), (1, 1), (0, 0)))
    mixed = jnp.zeros((count, lines, GRID, width), jnp.float32)
    for row in range(3):
        for col in range(3):
            mixed = mixed + conv_taps[row * 3 + col] * grid[:, row : row + lines, col : col + GRID]
    hidden = jax.nn.silu(mixed.reshape(count, length, width))
    query = product(hidden, query_proj) * HEAD_DIM ** (-0.5)
    keys = product(hidden, key_proj) * keep
    values = product(hidden, value_proj) * keep
    gates = (
        jax.nn.log_sigmoid(product(product(hidden, decay_down), decay_up) + decay_bias)
        / 16.0
        * keep
    )
    blocks = length // STRETCH

    def shaped(array):
        return array.reshape(count, blocks, STRETCH, HEADS, HEAD_DIM)

    query, keys, values, gates = (shaped(query), shaped(keys), shaped(values), shaped(gates))
    cumul = jnp.cumsum(gates, axis=2)
    group = math.gcd(count, max(1, 512 // length))

    def grouped(array):
        return array.reshape((count // group, group) + array.shape[1:])

    inner = lax.map(
        jax.checkpoint(lambda items: pair_mix(*items)),
        (grouped(query), grouped(keys), grouped(values), grouped(cumul)),
    )
    inner = inner.reshape(query.shape)
    decayed_query = query * jnp.exp(cumul)
    final = cumul[:, :, -1]
    carried = jnp.einsum(
        "ncshd,ncshe->nchde", keys * jnp.exp(final[:, :, None] - cumul), values, precision=HIGH
    )
    fades = jnp.exp(final)

    def advance(carry, items):
        total_fade, total_state = carry
        fade, state = items
        return (
            (fade * total_fade, fade[..., None] * total_state + state),
            (total_fade, total_state),
        )

    start = (jnp.ones_like(fades[:, 0]), jnp.zeros_like(carried[:, 0]))
    (dev_fade, dev_state), (pre_fade, pre_state) = lax.scan(
        advance, start, (jnp.moveaxis(fades, 1, 0), jnp.moveaxis(carried, 1, 0))
    )
    return (inner, decayed_query, pre_state, pre_fade, dev_fade, dev_state)


def tail(
    inner,
    decayed_query,
    pre_state,
    pre_fade,
    state_in,
    tokens,
    normed,
    modul,
    gate_proj,
    out_proj,
    mlp_up,
    mlp_down,
):
    count, length, width = tokens.shape
    shift_a, scale_a, gate_a, shift_b, scale_b, gate_b = jnp.split(modul, 6, axis=1)
    enter = pre_state + pre_fade[..., None] * state_in[None]
    outer = jnp.einsum("ncthd,cnhde->ncthe", decayed_query, enter, precision=HIGH)
    attended = (inner + outer).reshape(count, length, HEADS, HEAD_DIM)
    attended = attended * lax.rsqrt(jnp.mean(attended * attended, axis=-1, keepdims=True) + 1e-05)
    branch = product(
        attended.reshape(count, length, width) * jax.nn.silu(product(normed, gate_proj)), out_proj
    )
    middle = tokens + gate_a[:, None] * branch
    second = layer_norm(middle) * (1.0 + scale_b[:, None]) + shift_b[:, None]
    return middle + gate_b[:, None] * product(jax.nn.gelu(product(second, mlp_up)), mlp_down)


def body(
    tokens,
    valid_mask,
    timesteps,
    class_ids,
    time_first,
    time_second,
    class_table,
    ada_weight,
    ada_bias,
    conv_taps,
    query_proj,
    key_proj,
    value_proj,
    decay_down,
    decay_up,
    decay_bias,
    gate_proj,
    out_proj,
    mlp_up,
    mlp_down,
    cotangent,
):
    length = tokens.shape[1]

    def embed(first, second, table, weight, bias):
        return condition(timesteps, class_ids, first, second, table, weight, bias)

    modul, pull_embed = jax.vjp(embed, time_first, time_second, class_table, ada_weight, ada_bias)
    normed, pull_front = jax.vjp(front, tokens, modul)
    padded = extended(normed, (("seq", 1),), GRID)
    keep = valid_mask.astype(jnp.float32)[..., None]

    def mixer(pad_in, taps, q_weight, k_weight, v_weight, down_weight, up_weight, bias_in):
        return mixer_front(
            pad_in, keep, taps, q_weight, k_weight, v_weight, down_weight, up_weight, bias_in
        )

    parts, pull_mixer = jax.vjp(
        mixer, padded, conv_taps, query_proj, key_proj, value_proj, decay_down, decay_up, decay_bias
    )
    inner, decayed_query, pre_state, pre_fade, dev_fade, dev_state = parts
    state_in = carried_in(
        (dev_fade, dev_state),
        "seq",
        chain_join,
        (jnp.ones_like(dev_fade), jnp.zeros_like(dev_state)),
        False,
    )[1]
    block_out, pull_tail = jax.vjp(
        tail,
        inner,
        decayed_query,
        pre_state,
        pre_fade,
        state_in,
        tokens,
        normed,
        modul,
        gate_proj,
        out_proj,
        mlp_up,
        mlp_down,
    )
    (
        d_inner,
        d_query,
        d_pre_state,
        d_pre_fade,
        d_state,
        dx_tail,
        dn_tail,
        dmod_tail,
        g_gate,
        g_out,
        g_up,
        g_down,
    ) = pull_tail(cotangent)
    d_outgoing = carried_in(
        (dev_fade, d_state),
        "seq",
        chain_join,
        (jnp.ones_like(dev_fade), jnp.zeros_like(d_state)),
        True,
    )[1]
    d_dev_fade = jnp.sum(d_outgoing * state_in, axis=-1)
    pulled = pull_mixer((d_inner, d_query, d_pre_state, d_pre_fade, d_dev_fade, d_outgoing))
    d_pad = pulled[0]
    rims = jnp.concatenate([d_pad[:, :GRID], d_pad[:, -GRID:]], axis=1)
    beside_all = extended(rims, (("seq", 1),), GRID)
    d_normed = d_pad[:, GRID:-GRID] + dn_tail
    d_normed = d_normed + jnp.pad(beside_all[:, :GRID], ((0, 0), (0, length - GRID), (0, 0)))
    d_normed = d_normed + jnp.pad(beside_all[:, -GRID:], ((0, 0), (length - GRID, 0), (0, 0)))
    dx_front, dmod_front = pull_front(d_normed)
    tokens_grad = dx_tail + dx_front
    embed_grads = pull_embed(dmod_tail + dmod_front)
    first_grads = tuple(embed_grads) + tuple(pulled[1:])
    summed = lax.psum(first_grads + (g_gate, g_out, g_up, g_down), ("img", "seq"))
    return (
        block_out,
        tokens_grad,
        summed[0],
        summed[1],
        summed[2],
        summed[3],
        summed[4],
        summed[5],
        summed[6],
        summed[7],
        summed[8],
        summed[9],
        summed[10],
        summed[11],
        summed[12],
        summed[13],
        summed[14],
        summed[15],
    )


def solution(mesh):
    placed = (
        P("img", "seq", None),
        P("img", "seq"),
        P("img"),
        P("img"),
        P(),
        P(),
        P(),
        P(),
        P(),
        P(),
        P(),
        P(),
        P(),
        P(),
        P(),
        P(),
        P(),
        P(),
        P(),
        P(),
        P("img", "seq", None),
    )
    return jax.shard_map(
        body,
        mesh=mesh,
        in_specs=placed,
        out_specs=(
            P("img", "seq", None),
            P("img", "seq", None),
            P(),
            P(),
            P(),
            P(),
            P(),
            P(),
            P(),
            P(),
            P(),
            P(),
            P(),
            P(),
            P(),
            P(),
            P(),
            P(),
        ),
        check_vma=False,
    )
```

profile of v0, /device:TPU:0, one launch (start us, length us, event | category | flops | bytes accessed | tf_op | source)
XLA Modules:
  0.0 1686.3 jit_solution(18301640404507162143)
XLA Ops:
  54.4 8.6 divide_multiply_fusion
  158.7 7.7 fusion.55
  168.5 105.6 %while.81 = (s32[]{:T(128)}, f32[1,6,64]{2,1,0:T(8,128)S(1)}, f32[1,6,64,64]{3,2,1,0:T(8,128)}, f32[16,1,6,64]{3,2,1,0:T(8,128)}, f32[16,1,6,64,64]{4,3,2,1,0:T(...) while((s32[]{:T(128)}, f32[1,6,64]{2,1,0:T(8,128)S(1)}, ...), condition=%wide.region_5.6_spmd.clone, body=%wide.region_4.5_spmd.clone.sunk | while | flops 99459 | bytes 711314 | solution.py:142
  281.0 11.8 all-gather.1
  292.9 7.4 while.82
  305.6 8.5 fusion.38
  314.1 83.2 %multiply_reduce_fusion.2 = f32[16,64,64,6]{2,3,1,0:T(8,128)} fusion(f32[16,64,6,64]{3,1,2,0:T(8,128)} %copy.357, f32[16,64,6,64]{3,2,1,0:T(8,128)} %copy.356, f32[16,64,6,64]{3,1,2,0:T(8,128)} %copy.353, f32[16,64,6,64]{3,2,1,0:T(8,128)} %copy.351, pred[64,64]{1,0:T(8,128)(4,1)S(1)} %copy-done.111), kind=kLoop, calls=%fused_computation.36 | loop fusion | flops 150601728 | bytes 7868416 | tf_op jit(solution)/shard_map/jvp()/while/body/eval_jaxpr/reduce_sum | solution.py:76
  397.2 8.8 multiply_reduce_fusion.6
  432.0 10.6 fusion.91
  442.7 13.2 fusion.77
  455.9 13.1 fusion.53
  468.9 13.9 fusion.19
  482.8 11.6 fusion.173
  494.4 9.5 fusion.89
  525.4 6.9 fusion.134
  548.4 7.1 fusion.29
  555.4 7.6 multiply_reduce_fusion.3
  564.7 10.0 all-gather.2
  576.8 7.4 while.83
  588.1 154.1 %while.80 = (s32[]{:T(128)}, f32[1,6,64]{2,1,0:T(8,128)S(1)}, f32[1,6,64,64]{3,2,1,0:T(8,128)}, f32[16,1,6,64]{3,0,2,1:T(8,128)}, f32[16,1,6,64,64]{4,3,2,1,0:T(...) while((s32[]{:T(128)}, f32[1,6,64]{2,1,0:T(8,128)S(1)}, ...), condition=%wide.region_21.22_spmd, body=%wide.region_19.21_spmd.sunk | while | flops 99459 | bytes 1202857 | solution.py:142
  742.1 9.9 fusion.35
  752.0 7.8 fusion.33
  788.9 8.0 fusion.63
  801.1 253.6 %fusion.13 = (f32[16,64,6,64]{3,1,2,0:T(8,128)}, f32[16,64,6,64]{3,2,1,0:T(8,128)}, f32[16,64,6,64]{3,1,2,0:T(8,128)}, f32[16,64,64,6]{2,3,1,0:T(8,128)}, f32[16,64,6,64]{3,2,1,0:T(8,128)}) fusion(f32[16,64,6,64]{3,1,2,0:T(8,128)} %copy.410, f32[16,64,6,64]{3,2,1,0:T(8,128)S(1)} %copy-done.36, f32[16,64,64,6]{2,3,1,0:T(8,128)} %copy.408, ...), kind=kLoop, calls=%fused_computation.35 | loop fusion | flops 425852928 | bytes 15732736 | tf_op jit(solution)/shard_map/transpose(jvp())/while/body/eval_jaxpr/checkpoint/reduce_sum | solution.py:72
  1065.2 12.6 fusion.133
  1077.8 21.7 %broadcast_multiply_fusion.2 = (f32[1,16,64,6,64]{4,1,3,2,0:T(8,128)}, f32[1,16,64,6,64]{4,1,3,2,0:T(8,128)}, f32[1,16,64,6,64]{4,1,3,2,0:T(8,128)}, f32[1,16,64,6,64]{4,1,3,2,0:T(8,128)}, f32[1,16,64,6,64]{4,1,3,2,0:T(8,128)}) fusion(f32[16,64]{0,1:T(8,128)S(1)} %copy-done.69, f32[16,64,6,64]{3,1,2,0:T(8,128)} %get-tuple-element.880, ...), kind=kLoop, calls=%fused_computation.165 | loop fusion | flops 6291456 | bytes 23646208 | tf_op jit(solution)/shard_map/transpose(jvp())/mul | solution.py:102
  1128.4 7.9 fusion.175
  1195.1 7.7 fusion.177
  1212.0 7.7 fusion.178
  1242.4 7.1 fusion.167
  1273.7 116.7 %all-reduce.27.cloned.1.call-done = (f32[2304]{0:T(1024)}, f32[9,384]{1,0:T(8,128)}, f32[384,16]{0,1:T(8,128)}, f32[16,384]{1,0:T(8,128)}, f32[384]{0:T(512)}) async-done(((f32[2304]{0:T(1024)}, f32[9,384]{1,0:T(8,128)}, f32[384,16]{0,1:T(8,128)}, f32[16,384]{1,0:T(8,128)}, f32[384]{0:T(512)}), (f32[2304]{0:T(1024)}, f32[9,384]{1,0:T(8,128)}, f32[384,16]{0,1:T(8,128)}, f32[16,384]{1,0:T(8,128)}, ...) | async-done | bytes 73744 | tf_op jit(solution)/shard_map/psum | solution.py:273
  1390.4 269.6 %all-reduce.29.cloned.1.call-done = (f32[256,384]{1,0:T(8,128)}, f32[384,384]{1,0:T(8,128)}, f32[1000,384]{1,0:T(8,128)}, f32[384,2304]{1,0:T(8,128)}, f32[384,3...) async-done(((f32[256,384]{1,0:T(8,128)}, ...) | async-done | bytes 13725712 | tf_op jit(solution)/shard_map/psum | solution.py:273
  (709 shorter events, 706.8 us)
Async XLA Ops:
  7.2 14.7 copy-start
  16.5 8.5 copy-start.70
  27.3 21.4 %collective-permute-start.1 = (f32[1,64,384]{1,2,0:T(8,128)}, f32[1,64,384]{1,2,0:T(8,128)}, u32[]{:S(2)}, u32[]{:S(2)}) collective-permute-start(f32[1,64,384]{1,2,0:T(8,128)} %get-tuple-element.1026), channel_id=1, source_target_pairs={{1,0},{2,1},{3,2},{5,4},{6,5},{7,6},{9,8},{10,9},{11,10},{13,12},{... | collective-permute-start | bytes 294920 | tf_op jit(solution)/shard_map/ppermute | solution.py:24
  28.6 20.1 %collective-permute-start = (f32[1,64,384]{1,2,0:T(8,128)}, f32[1,64,384]{1,2,0:T(8,128)}, u32[]{:S(2)}, u32[]{:S(2)}) collective-permute-start(f32[1,64,384]{1,2,0:T(8,128)} %get-tuple-element.1027), channel_id=1, source_target_pairs={{0,1},{1,2},{2,3},{4,5},{5,6},{6,7},{8,9},{9,10},{10,11},{12,13},{... | collective-permute-start | bytes 294920 | tf_op jit(solution)/shard_map/ppermute | solution.py:23
  32.3 79.0 %copy-start.64 = (f32[1,1024]{1,0:T(1,128)}, f32[1,1024]{1,0:T(1,128)S(1)}, u32[]{:S(2)}) copy-start(f32[1,1024]{1,0:T(1,128)S(1)} %convert_element_type.14) | copy-start | bytes 12292
  37.2 17.2 %copy-start.95 = (f32[384]{0:T(512)}, f32[384]{0:T(512)S(1)}, u32[]{:S(2)}) copy-start(f32[384]{0:T(512)S(1)} %get-tuple-element.900) | copy-start | bytes 4612
  280.4 12.4 copy-start.68
  305.5 8.5 copy-start.111
  314.1 83.2 %copy-start.8 = (f32[16,64,6,64]{3,1,2,0:T(8,128)S(1)}, f32[16,64,6,64]{3,1,2,0:T(8,128)}, u32[]{:S(2)}) copy-start(f32[16,64,6,64]{3,1,2,0:T(8,128)} %copy.363) | copy-start | bytes 4718596
  431.3 63.1 %copy-start.9 = (f32[1,1024,384]{1,2,0:T(8,128)}, f32[1,1024,384]{1,2,0:T(8,128)S(1)}, u32[]{:S(2)}) copy-start(f32[1,1024,384]{1,2,0:T(8,128)S(1)} %get-tuple-element.1000) | copy-start | bytes 4718596
  432.0 10.6 copy-start.45
  432.0 10.6 copy-start.129
  442.6 13.2 copy-start.114
  742.1 9.9 copy-start.20
  742.1 9.9 copy-start.22
  801.1 253.6 %copy-start.5 = (f32[1,16,64,6,64]{2,4,3,1,0:T(8,128)S(1)}, f32[1,16,64,6,64]{2,4,3,1,0:T(8,128)}, u32[]{:S(2)}) copy-start(f32[1,16,64,6,64]{2,4,3,1,0:T(8,128)} %copy-done.4) | copy-start | bytes 4718596
  1065.2 12.6 copy-start.3
  1065.2 12.6 copy-start.66
  1065.2 12.6 copy-start.49
  1065.2 12.6 copy-start.69
  1211.9 9.0 copy-start.123
  1211.9 9.5 copy-start.122
  1212.0 10.1 copy-start.121
  1212.0 10.6 copy-start.120
  1224.8 12.3 copy-start.109
  1224.8 13.6 copy-start.110
  1224.8 17.6 %copy-start.71 = (f32[1024]{0:T(1024)S(1)}, f32[1024]{0:T(1024)}, u32[]{:S(2)}) copy-start(f32[1024]{0:T(1024)} %copy-done.70) | copy-start | bytes 12292
  1224.8 17.6 %copy-start.80 = (f32[384]{0:T(512)S(1)}, f32[384]{0:T(512)}, u32[]{:S(2)}) copy-start(f32[384]{0:T(512)} %copy-done.79) | copy-start | bytes 4612
  1231.3 11.1 collective-permute-start.3
  1232.6 9.8 collective-permute-start.2
  1257.5 132.9 %all-reduce.27.cloned.1.call-start = ((), (), s32[]{:S(2)}) async-start(), calls=%async_computation | async-start | bytes 176128 | tf_op jit(solution)/shard_map/psum | solution.py:273
  1261.9 398.0 %all-reduce.29.cloned.1.call-start = ((), (), s32[]{:S(2)}) async-start(), calls=%async_computation.1 | async-start | bytes 27451392 | tf_op jit(solution)/shard_map/psum | solution.py:273
  (108 other events, 411.5 us)
Sparse Core Ops, SparseCore 0:
  1265.9 124.4 all-reduce.26
  1398.5 261.3 all-reduce.28
where the time goes:
time: 1700 us; the launch traced here: 1690 us
  other arithmetic  566 us (33%)
  local copies, waits for them, and re-layouts  415 us (24%)
  waiting for transfers between devices  386 us (23%)
  matrix products  264 us (16%)
  blocking collectives  28.2 us (2%)
  between operations  17.1 us (1%)
    psum x2, waiting for transfers between devices, body(): lax.psum(first_grads + (g_gate, g_out, g_up, g_down), ('img', 'seq'))  386 us
    reduce_sum x1, other arithmetic, pair_mix(): diff = cumul[..., :, None, :, :] - cumul[..., None, :, :, :]  254 us
    dot_general x33, matrix products, product(): jnp.dot(left, right, precision=HIGH, preferred_element_type=jnp.float32)  192 us
    reduce_sum x1, other arithmetic, pair_mix(): jnp.sum(query[..., :, None, :, :] * keys[..., None, :, :, :] * weight, ax...  83.2 us
    dynamic_update_slice x64, local copies, waits for them, and re-layouts, mixer_front(): lax.scan(advance, start, (jnp.moveaxis(fades, 1, 0), jnp.moveaxis(carried...  68 us
    unnamed x297, local copies, waits for them, and re-layouts  56.7 us
    dynamic_slice x32, local copies, waits for them, and re-layouts, mixer_front(): lax.scan(advance, start, (jnp.moveaxis(fades, 1, 0), jnp.moveaxis(carried...  53.4 us
    reshape x11, local copies, waits for them, and re-layouts, shaped(): return array.reshape(count, blocks, STRETCH, HEADS, HEAD_DIM)  43.4 us
  transfers between devices with their start and end apart: 6, of which 2 were waited for; matrix products, arithmetic and copies ran while one was open for 2% of the time, Pallas kernels for 0%

commit v1 on v0

--- a/solution.py
+++ b/solution.py
@@ -270,7 +270,7 @@
     tokens_grad = dx_tail + dx_front
     embed_grads = pull_embed(dmod_tail + dmod_front)
     first_grads = tuple(embed_grads) + tuple(pulled[1:])
-    summed = lax.psum(first_grads + (g_gate, g_out, g_up, g_down), ("img", "seq"))
+    summed = lax.psum(lax.psum(first_grads + (g_gate, g_out, g_up, g_down), "seq"), "img")
     return (
         block_out,
         tokens_grad,

time: 1700 us -> 2100 us (1.24)
  waiting for transfers between devices: 386 us -> 790 us
    psum x2 -> x4, waiting for transfers between devices: 386 us -> 790 us  [the longest x2 508 us: body(): lax.psum(lax.psum(first_grads + (g_gate, g_out, g_up, g_down), 'seq'), 'i...]
  transfers between devices with their start and end apart: 6 -> 8, of which waited for: 2 -> 4; matrix products, arithmetic and copies ran while one was open for 2% -> 2% of each run, Pallas kernels for 0% -> 0%
where the time goes in v1:
time: 2100 us; the launch traced here: 2090 us
  waiting for transfers between devices  790 us (38%)
  other arithmetic  566 us (27%)
  local copies, waits for them, and re-layouts  415 us (20%)
  matrix products  264 us (13%)
  blocking collectives  28.2 us (1%)
    psum x2, waiting for transfers between devices, body(): lax.psum(lax.psum(first_grads + (g_gate, g_out, g_up, g_down), 'seq'), 'i...  508 us
    psum x2, waiting for transfers between devices, body(): lax.psum(first_grads + (g_gate, g_out, g_up, g_down), 'seq')  282 us
    reduce_sum x1, other arithmetic, pair_mix(): diff = cumul[..., :, None, :, :] - cumul[..., None, :, :, :]  254 us
    dot_general x33, matrix products, product(): jnp.dot(left, right, precision=HIGH, preferred_element_type=jnp.float32)  192 us
    reduce_sum x1, other arithmetic, pair_mix(): jnp.sum(query[..., :, None, :, :] * keys[..., None, :, :, :] * weight, ax...  83.2 us
    dynamic_update_slice x64, local copies, waits for them, and re-layouts, mixer_front(): lax.scan(advance, start, (jnp.moveaxis(fades, 1, 0), jnp.moveaxis(carried...  68 us
    unnamed x297, local copies, waits for them, and re-layouts  56.7 us
    dynamic_slice x32, local copies, waits for them, and re-layouts, mixer_front(): lax.scan(advance, start, (jnp.moveaxis(fades, 1, 0), jnp.moveaxis(carried...  53.4 us
  transfers between devices with their start and end apart: 8, of which 4 were waited for; matrix products, arithmetic and copies ran while one was open for 2% of the time, Pallas kernels for 0%

profile of v1, /device:TPU:0, one launch (start us, length us, event | category | flops | bytes accessed | tf_op | source)
XLA Modules:
  0.0 2089.5 jit_solution(7694720663115882120)
XLA Ops:
  54.4 8.6 divide_multiply_fusion
  158.8 7.7 fusion.55
  168.6 105.6 %while.81 = (s32[]{:T(128)}, f32[1,6,64]{2,1,0:T(8,128)S(1)}, f32[1,6,64,64]{3,2,1,0:T(8,128)}, f32[16,1,6,64]{3,2,1,0:T(8,128)}, f32[16,1,6,64,64]{4,3,2,1,0:T(...) while((s32[]{:T(128)}, f32[1,6,64]{2,1,0:T(8,128)S(1)}, ...), condition=%wide.region_5.6_spmd.clone, body=%wide.region_4.5_spmd.clone.sunk | while | flops 99459 | bytes 711314 | solution.py:142
  281.1 11.8 all-gather.1
  292.9 7.4 while.82
  305.6 8.5 fusion.38
  314.1 83.2 %multiply_reduce_fusion.2 = f32[16,64,64,6]{2,3,1,0:T(8,128)} fusion(f32[16,64,6,64]{3,1,2,0:T(8,128)} %copy.357, f32[16,64,6,64]{3,2,1,0:T(8,128)} %copy.356, f32[16,64,6,64]{3,1,2,0:T(8,128)} %copy.353, f32[16,64,6,64]{3,2,1,0:T(8,128)} %copy.351, pred[64,64]{1,0:T(8,128)(4,1)S(1)} %copy-done.111), kind=kLoop, calls=%fused_computation.36 | loop fusion | flops 150601728 | bytes 7868416 | tf_op jit(solution)/shard_map/jvp()/while/body/eval_jaxpr/reduce_sum | solution.py:76
  397.3 8.8 multiply_reduce_fusion.6
  432.1 10.6 fusion.91
  442.7 13.2 fusion.77
  455.9 13.1 fusion.53
  469.0 13.9 fusion.19
  482.8 11.6 fusion.173
  494.5 9.5 fusion.89
  555.4 7.6 multiply_reduce_fusion.3
  564.6 10.0 all-gather.2
  576.8 7.4 while.83
  588.0 154.0 %while.80 = (s32[]{:T(128)}, f32[1,6,64]{2,1,0:T(8,128)S(1)}, f32[1,6,64,64]{3,2,1,0:T(8,128)}, f32[16,1,6,64]{3,0,2,1:T(8,128)}, f32[16,1,6,64,64]{4,3,2,1,0:T(...) while((s32[]{:T(128)}, f32[1,6,64]{2,1,0:T(8,128)S(1)}, ...), condition=%wide.region_21.22_spmd, body=%wide.region_19.21_spmd.sunk | while | flops 99459 | bytes 1202857 | solution.py:142
  742.0 9.9 fusion.35
  751.8 7.8 fusion.33
  788.7 8.0 fusion.63
  800.9 253.6 %fusion.13 = (f32[16,64,6,64]{3,1,2,0:T(8,128)}, f32[16,64,6,64]{3,2,1,0:T(8,128)}, f32[16,64,6,64]{3,1,2,0:T(8,128)}, f32[16,64,64,6]{2,3,1,0:T(8,128)}, f32[16,64,6,64]{3,2,1,0:T(8,128)}) fusion(f32[16,64,6,64]{3,1,2,0:T(8,128)} %copy.410, f32[16,64,6,64]{3,2,1,0:T(8,128)S(1)} %copy-done.36, f32[16,64,64,6]{2,3,1,0:T(8,128)} %copy.408, ...), kind=kLoop, calls=%fused_computation.35 | loop fusion | flops 425852928 | bytes 15732736 | tf_op jit(solution)/shard_map/transpose(jvp())/while/body/eval_jaxpr/checkpoint/reduce_sum | solution.py:72
  1065.1 12.6 fusion.133
  1077.7 21.7 %broadcast_multiply_fusion.2 = (f32[1,16,64,6,64]{4,1,3,2,0:T(8,128)}, f32[1,16,64,6,64]{4,1,3,2,0:T(8,128)}, f32[1,16,64,6,64]{4,1,3,2,0:T(8,128)}, f32[1,16,64,6,64]{4,1,3,2,0:T(8,128)}, f32[1,16,64,6,64]{4,1,3,2,0:T(8,128)}) fusion(f32[16,64]{0,1:T(8,128)S(1)} %copy-done.69, f32[16,64,6,64]{3,1,2,0:T(8,128)} %get-tuple-element.880, ...), kind=kLoop, calls=%fused_computation.165 | loop fusion | flops 6291456 | bytes 23646208 | tf_op jit(solution)/shard_map/transpose(jvp())/mul | solution.py:102
  1128.2 7.9 fusion.175
  1195.0 7.7 fusion.177
  1211.8 7.7 fusion.178
  1242.2 7.1 fusion.167
  1262.7 32.1 %all-reduce.35.cloned.1.call-done = (f32[2304]{0:T(1024)}, f32[9,384]{1,0:T(8,128)}, f32[384,16]{0,1:T(8,128)}, f32[16,384]{1,0:T(8,128)}, f32[384]{0:T(512)}) async-done(((f32[2304]{0:T(1024)}, f32[9,384]{1,0:T(8,128)}, f32[384,16]{0,1:T(8,128)}, f32[16,384]{1,0:T(8,128)}, f32[384]{0:T(512)}), (f32[2304]{0:T(1024)}, f32[9,384]{1,0:T(8,128)}, f32[384,16]{0,1:T(8,128)}, f32[16,384]{1,0:T(8,128)}, ...) | async-done | bytes 73744 | tf_op jit(solution)/shard_map/psum | solution.py:273
  1294.9 249.9 %all-reduce.37.cloned.1.call-done = (f32[256,384]{1,0:T(8,128)}, f32[384,384]{1,0:T(8,128)}, f32[1000,384]{1,0:T(8,128)}, f32[384,2304]{1,0:T(8,128)}, f32[384,3...) async-done(((f32[256,384]{1,0:T(8,128)}, ...) | async-done | bytes 13725712 | tf_op jit(solution)/shard_map/psum | solution.py:273
  1555.6 63.8 %all-reduce.31.cloned.1.call-done = (f32[2304]{0:T(1024)}, f32[9,384]{1,0:T(8,128)}, f32[384,16]{0,1:T(8,128)}, f32[16,384]{1,0:T(8,128)}, f32[384]{0:T(512)}) async-done(((f32[2304]{0:T(1024)}, f32[9,384]{1,0:T(8,128)}, f32[384,16]{0,1:T(8,128)}, f32[16,384]{1,0:T(8,128)}, f32[384]{0:T(512)}), (f32[2304]{0:T(1024)}, f32[9,384]{1,0:T(8,128)}, f32[384,16]{0,1:T(8,128)}, f32[16,384]{1,0:T(8,128)}, ...) | async-done | bytes 73744 | tf_op jit(solution)/shard_map/psum | solution.py:273
  1619.4 444.0 %all-reduce.33.cloned.1.call-done = (f32[256,384]{1,0:T(8,128)}, f32[384,384]{1,0:T(8,128)}, f32[1000,384]{1,0:T(8,128)}, f32[384,2304]{1,0:T(8,128)}, f32[384,3...) async-done(((f32[256,384]{1,0:T(8,128)}, ...) | async-done | bytes 13725712 | tf_op jit(solution)/shard_map/psum | solution.py:273
  (715 shorter events, 720.6 us)
Async XLA Ops:
  7.2 14.7 copy-start
  27.3 21.4 %collective-permute-start.1 = (f32[1,64,384]{1,2,0:T(8,128)}, f32[1,64,384]{1,2,0:T(8,128)}, u32[]{:S(2)}, u32[]{:S(2)}) collective-permute-start(f32[1,64,384]{1,2,0:T(8,128)} %get-tuple-element.1042), channel_id=1, source_target_pairs={{1,0},{2,1},{3,2},{5,4},{6,5},{7,6},{9,8},{10,9},{11,10},{13,12},{... | collective-permute-start | bytes 294920 | tf_op jit(solution)/shard_map/ppermute | solution.py:24
  28.6 20.1 collective-permute-start
  32.3 79.1 %copy-start.64 = (f32[1,1024]{1,0:T(1,128)}, f32[1,1024]{1,0:T(1,128)S(1)}, u32[]{:S(2)}) copy-start(f32[1,1024]{1,0:T(1,128)S(1)} %convert_element_type.14) | copy-start | bytes 12292
  37.2 17.2 copy-start.95
  280.5 12.4 copy-start.68
  314.1 83.2 %copy-start.8 = (f32[16,64,6,64]{3,1,2,0:T(8,128)S(1)}, f32[16,64,6,64]{3,1,2,0:T(8,128)}, u32[]{:S(2)}) copy-start(f32[16,64,6,64]{3,1,2,0:T(8,128)} %copy.363) | copy-start | bytes 4718596
  431.4 63.1 %copy-start.9 = (f32[1,1024,384]{1,2,0:T(8,128)}, f32[1,1024,384]{1,2,0:T(8,128)S(1)}, u32[]{:S(2)}) copy-start(f32[1,1024,384]{1,2,0:T(8,128)S(1)} %get-tuple-element.1016) | copy-start | bytes 4718596
  432.0 10.6 copy-start.45
  432.1 10.6 copy-start.129
  442.7 13.2 copy-start.114
  742.0 9.9 copy-start.20
  742.0 9.9 copy-start.22
  800.9 253.6 %copy-start.5 = (f32[1,16,64,6,64]{2,4,3,1,0:T(8,128)S(1)}, f32[1,16,64,6,64]{2,4,3,1,0:T(8,128)}, u32[]{:S(2)}) copy-start(f32[1,16,64,6,64]{2,4,3,1,0:T(8,128)} %copy-done.4) | copy-start | bytes 4718596
  1065.0 12.6 copy-start.3
  1065.0 12.6 copy-start.66
  1065.0 12.6 copy-start.49
  1065.0 12.6 copy-start.69
  1211.7 8.9 copy-start.123
  1211.7 9.5 copy-start.122
  1211.7 10.0 copy-start.121
  1211.7 10.6 copy-start.120
  1224.6 12.3 copy-start.109
  1224.6 13.6 copy-start.110
  1224.6 17.6 copy-start.71
  1224.6 17.6 copy-start.80
  1231.1 11.1 collective-permute-start.3
  1232.4 9.8 collective-permute-start.2
  1257.3 37.6 %all-reduce.35.cloned.1.call-start = ((), (), s32[]{:S(2)}) async-start(), calls=%async_computation.2 | async-start | bytes 176128 | tf_op jit(solution)/shard_map/psum | solution.py:273
  1261.7 283.1 %all-reduce.37.cloned.1.call-start = ((), (), s32[]{:S(2)}) async-start(), calls=%async_computation.3 | async-start | bytes 27451392 | tf_op jit(solution)/shard_map/psum | solution.py:273
  1262.7 356.7 %all-reduce.31.cloned.1.call-start = ((), (), s32[]{:S(2)}) async-start(), calls=%async_computation | async-start | bytes 176128 | tf_op jit(solution)/shard_map/psum | solution.py:273
  1294.9 768.6 %all-reduce.33.cloned.1.call-start = ((), (), s32[]{:S(2)}) async-start(), calls=%async_computation.1 | async-start | bytes 27451392 | tf_op jit(solution)/shard_map/psum | solution.py:273
  (110 other events, 428.6 us)
Sparse Core Ops, SparseCore 0:
  1261.9 32.8 all-reduce.34
  1300.7 243.9 all-reduce.36
  1548.7 70.6 all-reduce.30
  1625.7 437.6 all-reduce.32
